TPU v7x, 32 devices: a whole 2x2x4 slice. The times are simulated.
32 devices in a mesh: energy: 16 (over z, x, core), mom: 2 (over y).
Axes of the slice: x: 2, y: 2, z: 4, core: 2. Of those that a mesh axis runs over, the one named last changes fastest.
Arguments:
- sigma_in: float32 [64, 2, 2, 256, 256], P('energy', 'mom'), may hold values from -0.1875 to 0.1875
- hamiltonian: float32 [2, 2, 256, 256], P('mom'), may hold values from -0.375 to 0.375
- coupling: float32 [2, 256, 256], P('mom'), may hold values from -0.1875 to 0.1875
- energies: float32 [64], replicated, may hold values from 1.4 to 2, as said below
- counts: int32 [64], replicated, may hold values from 2 to 4, as said below
- strengths: float32 [16], replicated, may hold values from 0.05625 to 0.1875
- offsets: int32 [16], replicated, may hold values from 0 to 1
Outputs:
- sigma_next: float32 [64, 2, 2, 256, 256], P('energy', 'mom')
Inputs may be any that keep to these rules, and one draw needn't show every extreme that they name: `energies`: increasing along the grid. `counts`: each point needs either 2 or 4 sweeps, and some point needs 4.
All inputs are finite; a program needn't handle non-finite values.
Results may differ from a plain program's by a relative error of at most 0.0003.
Values sent between devices are 32-bit elements; how exact they have to be, the bound alone decides.
A program may use at most 64 MiB of HBM per device.

v0:
```python
import jax
import jax.numpy as jnp
from jax import lax
from jax.sharding import PartitionSpec as P

PRECISE = lax.Precision.HIGHEST
MIX_RATE = 0.6
PHONON = 0.1
BROADENING = 0.02


def shifted(value, axis, steps):
    count = lax.axis_size(axis)
    pairs = [(source, (source + steps) % count) for source in range(count)]
    return lax.ppermute(value, axis, pairs)


def product(left_side, right_side):
    return jnp.dot(left_side, right_side, precision=PRECISE, preferred_element_type=jnp.float32)


def invert(matrix, energy, sweeps):
    identity = jnp.eye(matrix.shape[0], dtype=jnp.float32)

    def keep_going(carried):
        return carried[0] < sweeps

    def sweep(carried):
        estimate = carried[1]
        return (carried[0] + 1, 2.0 * estimate - product(estimate, product(matrix, estimate)))

    return lax.while_loop(keep_going, sweep, (jnp.int32(0), identity / energy))[1]


def solve_point(ham_block, coupling_block, sigma_pair, energy, sweeps):
    identity = jnp.eye(ham_block.shape[1], dtype=jnp.float32)
    left_matrix = energy * identity - ham_block[0] - sigma_pair[0]
    left_inverse = invert(left_matrix, energy, sweeps)
    inverse_coupled = product(left_inverse, coupling_block)
    coupled_inverse = product(coupling_block.T, left_inverse)
    right_matrix = (
        energy * identity
        - ham_block[1]
        - sigma_pair[1]
        - product(coupling_block.T, inverse_coupled)
    )
    right_green = invert(right_matrix, energy, sweeps)
    left_green = left_inverse + product(product(inverse_coupled, right_green), coupled_inverse)
    return jnp.stack([left_green, right_green])


def lorentz(offset):
    scaled = offset / BROADENING
    return 1.0 / (1.0 + scaled * scaled)


def build_kernel(row_energy, column_energy):
    spacing = row_energy[:, None] - column_energy[None, :]
    kernel = lorentz(spacing - PHONON) + lorentz(spacing + PHONON)
    return kernel / jnp.sum(kernel, axis=1, keepdims=True)


def body(sigma_in, hamiltonian, coupling, energies, counts, strengths, offsets):
    points = sigma_in.shape[0]
    order = sigma_in.shape[3]
    ranks = lax.axis_size("energy")
    moments = lax.axis_size("mom")
    my_rank = lax.axis_index("energy")
    own_energy = lax.dynamic_slice_in_dim(energies, my_rank * points, points)
    own_count = lax.dynamic_slice_in_dim(counts, my_rank * points, points)
    blocks = sigma_in[:, 0]

    def solve_held(held_point):
        return solve_point(hamiltonian[0], coupling[0], held_point[0], held_point[1], held_point[2])

    green_blocks = lax.map(solve_held, (blocks, own_energy, own_count))
    shift_index = jnp.arange(moments, dtype=jnp.int32)
    weights = jnp.sum(
        strengths[:, None] * (offsets[:, None] == shift_index[None, :]).astype(jnp.float32), axis=0
    )
    kernel = build_kernel(energies, energies)
    piece_width = 2 * order * order // ranks
    spread = green_blocks.reshape(points, ranks, moments, piece_width // moments)
    column = lax.all_to_all(spread, "energy", split_axis=1, concat_axis=0, tiled=True)[:, 0]
    rows_all = column.shape[0]
    flat_column = column.reshape(rows_all, -1)
    mixed_sum = weights[0] * flat_column
    for offset_step in range(1, moments):
        mixed_sum = mixed_sum + weights[offset_step] * shifted(flat_column, "mom", offset_step)
    sigma_part = product(kernel, mixed_sum).reshape(column.shape)
    result = lax.all_to_all(sigma_part[:, None], "energy", split_axis=0, concat_axis=1, tiled=True)
    sigma_new = result.reshape(sigma_in.shape)
    return (1.0 - MIX_RATE) * sigma_in + MIX_RATE * sigma_new


def solution(mesh):
    placed = (
        P("energy", "mom", None, None, None),
        P("mom", None, None, None),
        P("mom", None, None),
        P(),
        P(),
        P(),
        P(),
    )
    return jax.shard_map(
        body,
        mesh=mesh,
        in_specs=placed,
        out_specs=P("energy", "mom", None, None, None),
        check_vma=False,
    )
```

profile of v0, /device:TPU:1, one launch (start us, length us, event | category | flops | bytes accessed | tf_op | source)
XLA Modules:
  0.0 264.2 jit_solution(9605364366974160668)
XLA Ops:
  1.5 3.0 %copy.36 = f32[4,1,2,256,256]{3,4,2,0,1:T(8,128)} copy(f32[4,1,2,256,256]{4,3,2,1,0:T(8,128)} %param.13) | data formatting | bytes 4194304 | tf_op args[0]
  4.7 73.6 %while.32 = (s32[]{:T(128)}, f32[4,2,256,256]{3,2,1,0:T(8,128)}, f32[4]{0:T(128)S(1)}, s32[4]{0:T(128)S(1)}, f32[1,2,256,256]{2,3,1,0:T(8,128)S(1)}, /*index=5*/...) while((s32[]{:T(128)}, f32[4,2,256,256]{3,2,1,0:T(8,128)}, ...), condition=%wide.region_7.8_spmd, body=%wide.region_2.7_spmd.sunk | while | flops 1813118976 | bytes 13632415 | solution.py:76
  5.4 1.7 fusion.97
  8.5 3.8 %while.33 = (s32[]{:T(128)}, f32[256,256]{0,1:T(8,128)S(1)}, s32[]{:T(128)}, f32[256,256]{1,0:T(8,128)S(1)}, s32[]{:T(128)}) while((s32[]{:T(128)}, f32[256,256]{0,1:T(8,128)S(1)}, s32[]{:T(128)}, f32[256,256]{1,0:T(8,128)S(1)}, s32[]{:T(128)}) %tuple.63), condition=%wide.region_4.4_spmd, body=%wide.region_3.3_spmd.sunk | while | flops 402784256 | bytes 2097213 | solution.py:32
  12.9 2.2 fusion.99
  15.3 3.8 %while.34 = (s32[]{:T(128)}, f32[256,256]{0,1:T(8,128)S(1)}, s32[]{:T(128)}, f32[256,256]{1,0:T(8,128)S(1)}, s32[]{:T(128)}) while((s32[]{:T(128)}, f32[256,256]{0,1:T(8,128)S(1)}, s32[]{:T(128)}, f32[256,256]{1,0:T(8,128)S(1)}, s32[]{:T(128)}) %tuple.66), condition=%wide.region_6.6_spmd, body=%wide.region_5.5_spmd.sunk | while | flops 402784256 | bytes 2097213 | solution.py:32
  25.3 3.8 %while.33 = (s32[]{:T(128)}, f32[256,256]{0,1:T(8,128)S(1)}, s32[]{:T(128)}, f32[256,256]{1,0:T(8,128)S(1)}, s32[]{:T(128)}) while((s32[]{:T(128)}, f32[256,256]{0,1:T(8,128)S(1)}, s32[]{:T(128)}, f32[256,256]{1,0:T(8,128)S(1)}, s32[]{:T(128)}) %tuple.63), condition=%wide.region_4.4_spmd, body=%wide.region_3.3_spmd.sunk | while | flops 402784256 | bytes 2097213 | solution.py:32
  29.7 2.2 fusion.99
  32.1 3.8 %while.34 = (s32[]{:T(128)}, f32[256,256]{0,1:T(8,128)S(1)}, s32[]{:T(128)}, f32[256,256]{1,0:T(8,128)S(1)}, s32[]{:T(128)}) while((s32[]{:T(128)}, f32[256,256]{0,1:T(8,128)S(1)}, s32[]{:T(128)}, f32[256,256]{1,0:T(8,128)S(1)}, s32[]{:T(128)}) %tuple.66), condition=%wide.region_6.6_spmd, body=%wide.region_5.5_spmd.sunk | while | flops 402784256 | bytes 2097213 | solution.py:32
  42.1 3.8 %while.33 = (s32[]{:T(128)}, f32[256,256]{0,1:T(8,128)S(1)}, s32[]{:T(128)}, f32[256,256]{1,0:T(8,128)S(1)}, s32[]{:T(128)}) while((s32[]{:T(128)}, f32[256,256]{0,1:T(8,128)S(1)}, s32[]{:T(128)}, f32[256,256]{1,0:T(8,128)S(1)}, s32[]{:T(128)}) %tuple.63), condition=%wide.region_4.4_spmd, body=%wide.region_3.3_spmd.sunk | while | flops 402784256 | bytes 2097213 | solution.py:32
  46.5 2.2 fusion.99
  48.9 3.8 %while.34 = (s32[]{:T(128)}, f32[256,256]{0,1:T(8,128)S(1)}, s32[]{:T(128)}, f32[256,256]{1,0:T(8,128)S(1)}, s32[]{:T(128)}) while((s32[]{:T(128)}, f32[256,256]{0,1:T(8,128)S(1)}, s32[]{:T(128)}, f32[256,256]{1,0:T(8,128)S(1)}, s32[]{:T(128)}) %tuple.66), condition=%wide.region_6.6_spmd, body=%wide.region_5.5_spmd.sunk | while | flops 402784256 | bytes 2097213 | solution.py:32
  58.8 7.1 %while.33 = (s32[]{:T(128)}, f32[256,256]{0,1:T(8,128)S(1)}, s32[]{:T(128)}, f32[256,256]{1,0:T(8,128)S(1)}, s32[]{:T(128)}) while((s32[]{:T(128)}, f32[256,256]{0,1:T(8,128)S(1)}, s32[]{:T(128)}, f32[256,256]{1,0:T(8,128)S(1)}, s32[]{:T(128)}) %tuple.63), condition=%wide.region_4.4_spmd, body=%wide.region_3.3_spmd.sunk | while | flops 402784256 | bytes 2097213 | solution.py:32
  66.5 2.2 fusion.99
  68.9 7.1 %while.34 = (s32[]{:T(128)}, f32[256,256]{0,1:T(8,128)S(1)}, s32[]{:T(128)}, f32[256,256]{1,0:T(8,128)S(1)}, s32[]{:T(128)}) while((s32[]{:T(128)}, f32[256,256]{0,1:T(8,128)S(1)}, s32[]{:T(128)}, f32[256,256]{1,0:T(8,128)S(1)}, s32[]{:T(128)}) %tuple.66), condition=%wide.region_6.6_spmd, body=%wide.region_5.5_spmd.sunk | while | flops 402784256 | bytes 2097213 | solution.py:32
  78.3 2.6 reshape.35
  81.2 64.8 %all_to_all.24 = f32[4,16,2,4096]{3,2,0,1:T(2,128)S(1)} all-to-all(f32[4,16,2,4096]{3,2,0,1:T(2,128)S(1)} %copy.38), channel_id=1, replica_groups=mesh['energy'=16,'mom'=2] {'energy'}, dimensions={1} | all-to-all | bytes 4194304 | tf_op jit(solution)/shard_map/all_to_all | solution.py:84
  149.4 45.5 %collective-permute-done = f32[64,8192]{1,0:T(8,128)S(1)} collective-permute-done((f32[64,8192]{1,0:T(8,128)S(1)}, f32[64,8192]{1,0:T(8,128)S(1)}, u32[]{:S(2)}, u32[]{:S(2)}) %collective-permute-start) | collective-permute-done | bytes 2097184 | tf_op jit(solution)/shard_map/ppermute | solution.py:15
  194.9 3.2 %fusion.13 = f32[64,8192]{1,0:T(8,128)S(1)} fusion(f32[64,8192]{1,0:T(8,128)S(1)} %collective-permute-done, f32[64,8192]{1,0:T(8,128)S(1)} %bitcast.135, f32[]{:T(128)} %bitcast.17, f32[]{:T(128)} %bitcast.13, f32[64]{0:T(128)S(1)} %fusion.31, f32[64]{0:T(128)S(1)} %copy-done.3), kind=kOutput, calls=%fused_computation.23 | convolution fusion | flops 404279296 | bytes 6291976 | tf_op jit(solution)/shard_map/dot_general | solution.py:19
  198.1 2.8 %broadcast_in_dim_reshape.3 = f32[64,1,2,4096]{3,2,0,1:T(2,128)} reshape(f32[64,8192]{1,0:T(8,128)S(1)} %fusion.13) | data formatting | bytes 4194304 | tf_op jit(solution)/shard_map/broadcast_in_dim;reshape | solution.py:91
  200.8 52.6 %all_to_all.25 = f32[64,1,2,4096]{3,2,1,0:T(2,128)S(1)} all-to-all(f32[64,1,2,4096]{3,2,1,0:T(2,128)} %bitcast.137), channel_id=1, replica_groups=mesh['energy'=16,'mom'=2] {'energy'}, dimensions={0} | all-to-all | bytes 4194304 | tf_op jit(solution)/shard_map/all_to_all | solution.py:91
  253.4 1.9 broadcast_multiply_fusion
  256.8 4.2 %mul.86 = f32[4,1,2,256,256]{4,3,2,1,0:T(8,128)} reshape(f32[4,16,1,2,4096]{4,3,1,0,2:T(2,128)} %copy.40) | data formatting | bytes 4194304 | tf_op jit(solution)/shard_map/mul | solution.py:93
  261.0 3.2 %multiply_add_fusion = f32[4,1,2,256,256]{4,3,2,1,0:T(8,128)} fusion(f32[4,1,2,256,256]{4,3,2,1,0:T(8,128)} %mul.86, f32[4,1,2,256,256]{4,3,2,1,0:T(8,128)S(1)} %copy-done.1), kind=kLoop, calls=%fused_computation.27 | loop fusion | flops 1048576 | bytes 6291456 | tf_op jit(solution)/shard_map/add | solution.py:93
  (138 shorter events, 50.0 us)
Async XLA Ops:
  1.5 3.0 %copy-start.2 = (f32[1,2,256,256]{3,2,1,0:T(8,128)S(1)}, f32[1,2,256,256]{3,2,1,0:T(8,128)}, u32[]{:S(2)}) copy-start(f32[1,2,256,256]{3,2,1,0:T(8,128)} %param.14) | copy-start | bytes 1572868
  1.5 3.2 %copy-start = (f32[1,256,256]{2,1,0:T(8,128)S(1)}, f32[1,256,256]{2,1,0:T(8,128)}, u32[]{:S(2)}) copy-start(f32[1,256,256]{2,1,0:T(8,128)} %param.15) | copy-start | bytes 786436
  146.0 2.5 copy-start.4
  146.0 2.5 copy-start.5
  146.0 3.2 %copy-start.3 = (f32[64]{0:T(128)S(1)}, f32[64]{0:T(128)}, u32[]{:S(2)}) copy-start(f32[64]{0:T(128)} %param.16) | copy-start | bytes 772
  147.2 47.7 %collective-permute-start = (f32[64,8192]{1,0:T(8,128)S(1)}, f32[64,8192]{1,0:T(8,128)S(1)}, u32[]{:S(2)}, u32[]{:S(2)}) collective-permute-start(f32[64,8192]{1,0:T(8,128)S(1)} %bitcast.134), channel_id=1, source_target_pairs={{0,1},{1,0},{2,3},{3,2},{4,5},{5,4},{6,7},{7,6},{8,9},{9,8},{10,11... | collective-permute-start | bytes 6291464 | tf_op jit(solution)/shard_map/ppermute | solution.py:15
  256.8 4.2 %copy-start.1 = (f32[4,1,2,256,256]{4,3,2,1,0:T(8,128)S(1)}, f32[4,1,2,256,256]{4,3,2,1,0:T(8,128)}, u32[]{:S(2)}) copy-start(f32[4,1,2,256,256]{4,3,2,1,0:T(8,128)} %param.13) | copy-start | bytes 6291460
where the time goes:
time: 262 us; the launch traced here: 264 us
  blocking collectives  117 us (45%)
  waiting for transfers between devices  45.5 us (17%)
  matrix products  39.5 us (15%)
  local copies, waits for them, and re-layouts  25.2 us (10%)
  loops' own time  19.8 us (8%)
  other arithmetic  15.5 us (6%)
    all_to_all x1, blocking collectives, body(): lax.all_to_all(spread, 'energy', split_axis=1, concat_axis=0, tiled=True)  64.8 us
    all_to_all x1, blocking collectives, body(): lax.all_to_all(sigma_part[:, None], 'energy', split_axis=0, concat_axis=1...  52.6 us
    ppermute x1, waiting for transfers between devices, shifted(): return lax.ppermute(value, axis, pairs)  45.5 us
    dot_general x61, matrix products, product(): jnp.dot(left_side, right_side, precision=PRECISE, preferred_element_type=...  39.5 us
    another operation x8, loops' own time, invert(): lax.while_loop(keep_going, sweep, (jnp.int32(0), identity / energy))[1]  16.5 us
    sub x4, other arithmetic, solve_point(): left_matrix = energy * identity - ham_block[0] - sigma_pair[0]  6.66 us
    mul x2, local copies, waits for them, and re-layouts, body(): return (1.0 - MIX_RATE) * sigma_in + MIX_RATE * sigma_new  5.67 us
  transfers between devices with their start and end apart: 1, of which 1 were waited for; matrix products, arithmetic and copies ran while one was open for 0% of the time, Pallas kernels for 0%

commit v1 on v0

--- a/solution.py
+++ b/solution.py
@@ -1,6 +1,10 @@
+import functools
+
 import jax
 import jax.numpy as jnp
 from jax import lax
+from jax.experimental import pallas as pl
+from jax.experimental.pallas import tpu as pltpu
 from jax.sharding import PartitionSpec as P
 
 PRECISE = lax.Precision.HIGHEST
@@ -60,7 +64,7 @@
     return kernel / jnp.sum(kernel, axis=1, keepdims=True)
 
 
-def body(sigma_in, hamiltonian, coupling, energies, counts, strengths, offsets):
+def plain_body(sigma_in, hamiltonian, coupling, energies, counts, strengths, offsets):
     points = sigma_in.shape[0]
     order = sigma_in.shape[3]
     ranks = lax.axis_size("energy")
@@ -93,6 +97,244 @@
     return (1.0 - MIX_RATE) * sigma_in + MIX_RATE * sigma_new
 
 
+SUBLANES = 8
+TOGETHER = 2
+MESH_ID = pl.DeviceIdType.MESH
+
+
+def split(value):
+    high = value.astype(jnp.bfloat16)
+    return high, (value - high.astype(jnp.float32)).astype(jnp.bfloat16)
+
+
+def left_parts(value):
+    high, low = split(value)
+    return jnp.concatenate([high, low, high], axis=1)
+
+
+def right_parts(value):
+    high, low = split(value)
+    return jnp.concatenate([high, high, low], axis=0)
+
+
+def multiply(left_side, right_side):
+    return jnp.dot(left_side, right_side, preferred_element_type=jnp.float32)
+
+
+def series(ratios, energies, counts, identity):
+    order = identity.shape[0]
+    squares = [multiply(left_parts(r), right_parts(r)) for r in ratios]
+    totals = [identity + r for r in ratios]
+    for sweep in (1, 2, 3):
+        rights = [right_parts(s) for s in squares]
+        if sweep < 3:
+            both = [
+                multiply(jnp.concatenate([left_parts(t), left_parts(s)], axis=0), q)
+                for t, s, q in zip(totals, squares, rights)
+            ]
+            added = [b[:order] for b in both]
+            squares = [b[order:] for b in both]
+        else:
+            added = [multiply(left_parts(t), q) for t, q in zip(totals, rights)]
+        totals = [jnp.where(sweep < c, t + a, t) for t, a, c in zip(totals, added, counts)]
+    return [t * (1.0 / e) for t, e in zip(totals, energies)]
+
+
+def kernel(
+    ranks, moments, points, order, held,
+    energy_ref, count_ref, strength_ref, offset_ref, sigma_ref, ham_ref, coupling_ref,
+    out_ref,
+    green, gathered, mixed_out, wide, across, across_t,
+    send_first, recv_first, send_second, recv_second,
+):
+    devices = ranks * moments
+    total = ranks * points
+    my_rank = lax.axis_index("energy")
+    my_moment = lax.axis_index("mom")
+    me = my_rank * moments + my_moment
+    barrier = pltpu.get_barrier_semaphore()
+
+    def greet(index, carried):
+        other = lax.rem(me + index, devices)
+        pl.semaphore_signal(
+            barrier, inc=1,
+            device_id={"energy": other // moments, "mom": lax.rem(other, moments)},
+            device_id_type=MESH_ID,
+        )
+        return carried
+
+    lax.fori_loop(1, devices, greet, 0)
+
+    span = total * SUBLANES
+    column = lax.broadcasted_iota(jnp.int32, (SUBLANES, span), 1)
+    lane_slot = lax.rem(column, SUBLANES)
+    lane_point = lax.div(column, SUBLANES)
+    same = lane_slot == lax.broadcasted_iota(jnp.int32, (SUBLANES, span), 0)
+
+    def place(index, carried):
+        return jnp.where(lane_point == index, energy_ref[index], carried)
+
+    column_energy = lax.fori_loop(0, total, place, jnp.zeros((SUBLANES, span), jnp.float32))
+
+    def build(index, carried):
+        spacing = energy_ref[index] - column_energy
+        row = lorentz(spacing - PHONON) + lorentz(spacing + PHONON)
+        row = jnp.where(same, row, 0.0)
+        row = row / jnp.sum(row, axis=1, keepdims=True)
+        wide[pl.ds(pl.multiple_of(index * SUBLANES, SUBLANES), SUBLANES), :] = row
+        return carried
+
+    lax.fori_loop(0, total, build, 0)
+    weights = []
+    for step in range(moments):
+        weight = jnp.float32(0.0)
+        for transfer in range(strength_ref.shape[0]):
+            weight = weight + jnp.where(offset_ref[transfer] == step, strength_ref[transfer], 0.0)
+        weights.append(weight)
+
+    across[...] = right_parts(coupling_ref[...])
+    across_t[...] = left_parts(coupling_ref[...].T)
+    row_index = lax.broadcasted_iota(jnp.int32, (order, order), 0)
+    identity = (row_index == lax.broadcasted_iota(jnp.int32, (order, order), 1)).astype(jnp.float32)
+    pl.semaphore_wait(barrier, devices - 1)
+
+    half = devices // 2
+
+    def first_copy(point, other):
+        return pltpu.make_async_remote_copy(
+            src_ref=green.at[point, pl.ds(other * held, held)],
+            dst_ref=gathered.at[my_moment, :, my_rank * points + point],
+            send_sem=send_first,
+            recv_sem=recv_first,
+            device_id={"energy": other // moments, "mom": lax.rem(other, moments)},
+            device_id_type=MESH_ID,
+        )
+
+    def solve(group, carried):
+        chosen = [group * TOGETHER + index for index in range(TOGETHER)]
+        energies = [energy_ref[my_rank * points + point] for point in chosen]
+        counts = [count_ref[my_rank * points + point] for point in chosen]
+        ratios = [(ham_ref[0] + sigma_ref[point, 0]) * (1.0 / e) for point, e in zip(chosen, energies)]
+        left_inverses = series(ratios, energies, counts, identity)
+        coupled = [multiply(left_parts(x), across[...]) for x in left_inverses]
+        backs = [multiply(across_t[...], right_parts(x)) for x in left_inverses]
+        folds = [multiply(across_t[...], right_parts(x)) for x in coupled]
+        ratios = [
+            (ham_ref[1] + sigma_ref[point, 1] + fold) * (1.0 / e)
+            for point, e, fold in zip(chosen, energies, folds)
+        ]
+        right_greens = series(ratios, energies, counts, identity)
+        inner = [multiply(left_parts(c), right_parts(x)) for c, x in zip(coupled, right_greens)]
+        left_greens = [
+            x + multiply(left_parts(i), right_parts(b)) for x, i, b in zip(left_inverses, inner, backs)
+        ]
+        tiles = order // SUBLANES
+        for point, left_green, right_green in zip(chosen, left_greens, right_greens):
+            green[point, :tiles] = left_green.reshape(tiles, SUBLANES, order)
+            green[point, tiles:] = right_green.reshape(tiles, SUBLANES, order)
+        for point in chosen:
+            pltpu.make_async_copy(
+                green.at[point, pl.ds(me * held, held)],
+                gathered.at[my_moment, :, my_rank * points + point],
+                recv_first,
+            ).start()
+
+            def send(index, inner_carried, point=point):
+                away = (index + 1) // 2
+                offset = half + away * (2 * lax.rem(index, 2) - 1)
+                first_copy(point, lax.rem(me + offset, devices)).start()
+                return inner_carried
+
+            lax.fori_loop(0, devices - 1, send, 0)
+        return carried
+
+    lax.fori_loop(0, points // TOGETHER, solve, 0)
+
+    pltpu.make_async_copy(gathered, gathered, recv_first).wait()
+
+    wide_parts = left_parts(wide[...])
+    for turn in range(moments):
+        moment = lax.rem(my_moment + 1 + turn, moments)
+        for piece in range(held):
+            scattered = weights[0] * gathered[moment, piece]
+            for step in range(1, moments):
+                source = lax.rem(moment - step + moments, moments)
+                scattered = scattered + weights[step] * gathered[source, piece]
+            result = multiply(wide_parts, right_parts(scattered.reshape(span, order)))
+            mixed_out[moment, piece] = result.reshape(total, SUBLANES, order)
+
+            def give_back(index, carried, moment=moment, piece=piece):
+                away = (index + 1) // 2
+                offset = ranks // 2 + away * (2 * lax.rem(index, 2) - 1)
+                rank = lax.rem(my_rank + offset, ranks)
+                pltpu.make_async_remote_copy(
+                    src_ref=mixed_out.at[moment, piece, pl.ds(rank * points, points)],
+                    dst_ref=out_ref.at[:, me * held + piece],
+                    send_sem=send_second,
+                    recv_sem=recv_second,
+                    device_id={"energy": rank, "mom": moment},
+                    device_id_type=MESH_ID,
+                ).start()
+                return carried
+
+            if turn < moments - 1:
+                lax.fori_loop(0, ranks, give_back, 0)
+            else:
+                lax.fori_loop(0, ranks - 1, give_back, 0)
+                pltpu.make_async_copy(
+                    mixed_out.at[my_moment, piece, pl.ds(my_rank * points, points)],
+                    out_ref.at[:, me * held + piece],
+                    recv_second,
+                ).start()
+
+    pltpu.make_async_copy(out_ref, out_ref, recv_second).wait()
+    sent = green.at[:, pl.ds(0, (devices - 1) * held)]
+    pltpu.make_async_copy(sent, sent, send_first).wait()
+    pltpu.make_async_copy(sent, sent, send_second).wait()
+
+
+def fused_body(sigma_in, hamiltonian, coupling, energies, counts, strengths, offsets):
+    points, order = sigma_in.shape[0], sigma_in.shape[3]
+    ranks = lax.axis_size("energy")
+    moments = lax.axis_size("mom")
+    tiles = 2 * order // SUBLANES
+    held = tiles // (ranks * moments)
+    span = ranks * points * SUBLANES
+    smem = pl.BlockSpec(memory_space=pltpu.SMEM)
+    vmem = pl.BlockSpec(memory_space=pltpu.VMEM)
+    sigma_new = pl.pallas_call(
+        functools.partial(kernel, ranks, moments, points, order, held),
+        out_shape=jax.ShapeDtypeStruct((points, tiles, SUBLANES, order), jnp.float32),
+        in_specs=[smem] * 4 + [vmem] * 3,
+        out_specs=pl.BlockSpec(memory_space=pl.ANY),
+        scratch_shapes=[
+            pltpu.VMEM((points, tiles, SUBLANES, order), jnp.float32),
+            pltpu.VMEM((moments, held, ranks * points, SUBLANES, order), jnp.float32),
+            pltpu.VMEM((moments, held, ranks * points, SUBLANES, order), jnp.float32),
+            pltpu.VMEM((span, span), jnp.float32),
+            pltpu.VMEM((3 * order, order), jnp.bfloat16),
+            pltpu.VMEM((order, 3 * order), jnp.bfloat16),
+            pltpu.SemaphoreType.DMA,
+            pltpu.SemaphoreType.DMA,
+            pltpu.SemaphoreType.DMA,
+            pltpu.SemaphoreType.DMA,
+        ],
+        compiler_params=pltpu.CompilerParams(
+            collective_id=0, has_side_effects=True, vmem_limit_bytes=60 * 1024 * 1024
+        ),
+        name="green_and_scatter",
+    )(energies, counts, strengths, offsets, sigma_in[:, 0], hamiltonian[0], coupling[0])
+    return (1.0 - MIX_RATE) * sigma_in + MIX_RATE * sigma_new.reshape(sigma_in.shape)
+
+
+def body(sigma_in, hamiltonian, coupling, energies, counts, strengths, offsets):
+    devices = lax.axis_size("energy") * lax.axis_size("mom")
+    tiles = 2 * sigma_in.shape[3] // SUBLANES
+    fits = tiles % devices == 0 and devices % 2 == 0 and sigma_in.shape[0] % TOGETHER == 0
+    chosen = fused_body if fits else plain_body
+    return chosen(sigma_in, hamiltonian, coupling, energies, counts, strengths, offsets)
+
+
 def solution(mesh):
     placed = (
         P("energy", "mom", None, None, None),

time: 262 us -> 115 us (0.44); the launches traced: 264 us -> 113 us
  blocking collectives: 117 us -> 0 us
  Pallas kernels: 0 us -> 109 us
  waiting for transfers between devices: 45.5 us -> 0 us
  matrix products: 39.5 us -> 0 us
  local copies, waits for them, and re-layouts: 25.2 us -> 0.25 us
  loops' own time: 19.8 us -> 0 us
  other arithmetic: 15.5 us -> 3.63 us
    all_to_all x2 -> x0, blocking collectives: 117 us -> none  [the longest x1 64.8 us: body(): lax.all_to_all(spread, 'energy', split_axis=1, concat_axis=0, tiled=True)]
    pallas_call x0 -> x1, Pallas kernels: none -> 109 us  [fused_body(): pl.pallas_call(functools.partial(kernel, ranks, moments, points, order, h...]
    ppermute x1 -> x0, waiting for transfers between devices: 45.5 us -> none  [shifted(): return lax.ppermute(value, axis, pairs)]
    dot_general x61 -> x0, matrix products: 39.5 us -> none  [product(): jnp.dot(left_side, right_side, precision=PRECISE, preferred_element_type=...]
    another operation x9 -> x0, loops' own time: 19.8 us -> none  [the longest x8 16.5 us: invert(): lax.while_loop(keep_going, sweep, (jnp.int32(0), identity / energy))[1]]
    sub x4 -> x0, other arithmetic: 6.66 us -> none  [solve_point(): left_matrix = energy * identity - ham_block[0] - sigma_pair[0]]
    dynamic_slice x10 -> x0, local copies, waits for them, and re-layouts: 6.39 us -> none  [the longest x8 4.94 us: body(): green_blocks = lax.map(solve_held, (blocks, own_energy, own_count))]
    mul x2 -> x0, local copies, waits for them, and re-layouts: 5.67 us -> none  [body(): return (1.0 - MIX_RATE) * sigma_in + MIX_RATE * sigma_new]
  transfers between devices with their start and end apart: 1 -> 0, of which waited for: 1 -> 0; matrix products, arithmetic and copies ran while one was open for 0% -> 0% of each run, Pallas kernels for 0% -> 0%
where the time goes in v1:
time: 115 us; the launch traced here: 113 us
  Pallas kernels  109 us (95%)
  other arithmetic  3.63 us (3%)
    pallas_call x1, Pallas kernels, fused_body(): pl.pallas_call(functools.partial(kernel, ranks, moments, points, order, h...  109 us

profile of v1, /device:TPU:1, one launch (start us, length us, event | category | flops | bytes accessed | tf_op | source)
XLA Modules:
  0.0 113.1 jit_solution(704226307536475082)
XLA Ops:
  0.0 109.2 %green_and_scatter.1 = f32[4,64,8,256]{3,2,1,0:T(8,128)} custom-call(f32[64]{0:T(128)} %energy_ref.1, s32[64]{0:T(128)} %count_ref.1, f32[16]{0:T(128)} %strength_ref.1, s32[16]{0:T(128)} %offset_ref.1, f32[4,2,256,256]{3,2,1,0:T(8,128)} %bitcast.6, f32[2,256,256]{2,1,0:T(8,128)} %bitcast.8, f32[256,256]{1,0:T(8,128)} %bitcast.9), custom_call_target="tpu_custom_call" | custom-call | tf_op jit(solution)/shard_map/green_and_scatter/pallas_call | solution.py:305
  109.2 0.0 copy-start
  109.2 2.0 %broadcast_multiply_fusion = f32[4,64,8,256]{3,2,1,0:T(8,128)S(1)} fusion(f32[4,64,8,256]{3,2,1,0:T(8,128)} %green_and_scatter.1), kind=kLoop, calls=%fused_computation.1 | loop fusion | flops 524288 | bytes 4194304 | tf_op jit(solution)/shard_map/mul | solution.py:327
  111.1 0.2 copy-done
  111.4 1.7 %multiply_add_fusion = f32[4,1,2,256,256]{4,3,2,1,0:T(8,128)} fusion(f32[4,1,2,256,256]{4,3,2,1,0:T(8,128)S(1)} %bitcast.7, f32[4,1,2,256,256]{4,3,2,1,0:T(8,128)S(1)} %copy-done), kind=kLoop, calls=%fused_computation | loop fusion | flops 1048576 | bytes 6291456 | tf_op jit(solution)/shard_map/add | solution.py:327
Async XLA Ops:
  109.2 2.2 %copy-start = (f32[4,1,2,256,256]{4,3,2,1,0:T(8,128)S(1)}, f32[4,1,2,256,256]{4,3,2,1,0:T(8,128)}, u32[]{:S(2)}) copy-start(f32[4,1,2,256,256]{4,3,2,1,0:T(8,128)} %param.7) | copy-start | bytes 6291460

commit v2 on v1

--- a/solution.py
+++ b/solution.py
@@ -98,7 +98,7 @@
 
 
 SUBLANES = 8
-TOGETHER = 2
+TOGETHER = 1
 MESH_ID = pl.DeviceIdType.MESH
 
 
@@ -165,50 +165,30 @@
 
     lax.fori_loop(1, devices, greet, 0)
 
-    span = total * SUBLANES
-    column = lax.broadcasted_iota(jnp.int32, (SUBLANES, span), 1)
-    lane_slot = lax.rem(column, SUBLANES)
-    lane_point = lax.div(column, SUBLANES)
-    same = lane_slot == lax.broadcasted_iota(jnp.int32, (SUBLANES, span), 0)
-
-    def place(index, carried):
-        return jnp.where(lane_point == index, energy_ref[index], carried)
-
-    column_energy = lax.fori_loop(0, total, place, jnp.zeros((SUBLANES, span), jnp.float32))
-
-    def build(index, carried):
-        spacing = energy_ref[index] - column_energy
-        row = lorentz(spacing - PHONON) + lorentz(spacing + PHONON)
-        row = jnp.where(same, row, 0.0)
-        row = row / jnp.sum(row, axis=1, keepdims=True)
-        wide[pl.ds(pl.multiple_of(index * SUBLANES, SUBLANES), SUBLANES), :] = row
-        return carried
-
-    lax.fori_loop(0, total, build, 0)
-    weights = []
-    for step in range(moments):
-        weight = jnp.float32(0.0)
-        for transfer in range(strength_ref.shape[0]):
-            weight = weight + jnp.where(offset_ref[transfer] == step, strength_ref[transfer], 0.0)
-        weights.append(weight)
-
     across[...] = right_parts(coupling_ref[...])
     across_t[...] = left_parts(coupling_ref[...].T)
     row_index = lax.broadcasted_iota(jnp.int32, (order, order), 0)
     identity = (row_index == lax.broadcasted_iota(jnp.int32, (order, order), 1)).astype(jnp.float32)
-    pl.semaphore_wait(barrier, devices - 1)
-
-    half = devices // 2
-
-    def first_copy(point, other):
-        return pltpu.make_async_remote_copy(
-            src_ref=green.at[point, pl.ds(other * held, held)],
-            dst_ref=gathered.at[my_moment, :, my_rank * points + point],
-            send_sem=send_first,
-            recv_sem=recv_first,
-            device_id={"energy": other // moments, "mom": lax.rem(other, moments)},
-            device_id_type=MESH_ID,
-        )
+
+    def place_of(other):
+        return {"energy": other // moments, "mom": lax.rem(other, moments)}
+
+    def give_first(source, landing, piece):
+        pltpu.make_async_copy(source(me), landing, recv_first.at[piece]).start()
+
+        def give(index, carried):
+            other = lax.rem(me + index, devices)
+            pltpu.make_async_remote_copy(
+                src_ref=source(other),
+                dst_ref=landing,
+                send_sem=send_first,
+                recv_sem=recv_first.at[piece],
+                device_id=place_of(other),
+                device_id_type=MESH_ID,
+            ).start()
+            return carried
+
+        lax.fori_loop(1, devices, give, 0)
 
     def solve(group, carried):
         chosen = [group * TOGETHER + index for index in range(TOGETHER)]
@@ -232,30 +212,55 @@
         for point, left_green, right_green in zip(chosen, left_greens, right_greens):
             green[point, :tiles] = left_green.reshape(tiles, SUBLANES, order)
             green[point, tiles:] = right_green.reshape(tiles, SUBLANES, order)
+
+        @pl.when(group == 0)
+        def _():
+            pl.semaphore_wait(barrier, devices - 1)
+
         for point in chosen:
-            pltpu.make_async_copy(
-                green.at[point, pl.ds(me * held, held)],
-                gathered.at[my_moment, :, my_rank * points + point],
-                recv_first,
-            ).start()
-
-            def send(index, inner_carried, point=point):
-                away = (index + 1) // 2
-                offset = half + away * (2 * lax.rem(index, 2) - 1)
-                first_copy(point, lax.rem(me + offset, devices)).start()
-                return inner_carried
-
-            lax.fori_loop(0, devices - 1, send, 0)
+            landing = gathered.at[my_moment, 0, my_rank * points + point]
+            give_first(lambda other: green.at[point, other * held], landing, 0)
         return carried
 
     lax.fori_loop(0, points // TOGETHER, solve, 0)
 
-    pltpu.make_async_copy(gathered, gathered, recv_first).wait()
+    for piece in range(1, held):
+        landing = gathered.at[my_moment, piece, pl.ds(my_rank * points, points)]
+        give_first(lambda other: green.at[:, other * held + piece], landing, piece)
+
+    span = total * SUBLANES
+    column = lax.broadcasted_iota(jnp.int32, (SUBLANES, span), 1)
+    lane_slot = lax.rem(column, SUBLANES)
+    lane_point = lax.div(column, SUBLANES)
+    same = lane_slot == lax.broadcasted_iota(jnp.int32, (SUBLANES, span), 0)
+
+    def place(index, carried):
+        return jnp.where(lane_point == index, energy_ref[index], carried)
+
+    column_energy = lax.fori_loop(0, total, place, jnp.zeros((SUBLANES, span), jnp.float32))
+
+    def build(index, carried):
+        spacing = energy_ref[index] - column_energy
+        row = lorentz(spacing - PHONON) + lorentz(spacing + PHONON)
+        row = jnp.where(same, row, 0.0)
+        row = row * (MIX_RATE / jnp.sum(row, axis=1, keepdims=True))
+        wide[pl.ds(pl.multiple_of(index * SUBLANES, SUBLANES), SUBLANES), :] = row
+        return carried
+
+    lax.fori_loop(0, total, build, 0)
+    weights = []
+    for step in range(moments):
+        weight = jnp.float32(0.0)
+        for transfer in range(strength_ref.shape[0]):
+            weight = weight + jnp.where(offset_ref[transfer] == step, strength_ref[transfer], 0.0)
+        weights.append(weight)
 
     wide_parts = left_parts(wide[...])
-    for turn in range(moments):
-        moment = lax.rem(my_moment + 1 + turn, moments)
-        for piece in range(held):
+    for piece in range(held):
+        arrived = gathered.at[:, piece]
+        pltpu.make_async_copy(arrived, arrived, recv_first.at[piece]).wait()
+        for turn in range(moments):
+            moment = lax.rem(my_moment + 1 + turn, moments)
             scattered = weights[0] * gathered[moment, piece]
             for step in range(1, moments):
                 source = lax.rem(moment - step + moments, moments)
@@ -264,9 +269,7 @@
             mixed_out[moment, piece] = result.reshape(total, SUBLANES, order)
 
             def give_back(index, carried, moment=moment, piece=piece):
-                away = (index + 1) // 2
-                offset = ranks // 2 + away * (2 * lax.rem(index, 2) - 1)
-                rank = lax.rem(my_rank + offset, ranks)
+                rank = lax.rem(my_rank + index, ranks)
                 pltpu.make_async_remote_copy(
                     src_ref=mixed_out.at[moment, piece, pl.ds(rank * points, points)],
                     dst_ref=out_ref.at[:, me * held + piece],
@@ -280,7 +283,7 @@
             if turn < moments - 1:
                 lax.fori_loop(0, ranks, give_back, 0)
             else:
-                lax.fori_loop(0, ranks - 1, give_back, 0)
+                lax.fori_loop(1, ranks, give_back, 0)
                 pltpu.make_async_copy(
                     mixed_out.at[my_moment, piece, pl.ds(my_rank * points, points)],
                     out_ref.at[:, me * held + piece],
@@ -315,7 +318,7 @@
             pltpu.VMEM((3 * order, order), jnp.bfloat16),
             pltpu.VMEM((order, 3 * order), jnp.bfloat16),
             pltpu.SemaphoreType.DMA,
-            pltpu.SemaphoreType.DMA,
+            pltpu.SemaphoreType.DMA((held,)),
             pltpu.SemaphoreType.DMA,
             pltpu.SemaphoreType.DMA,
         ],
@@ -324,7 +327,7 @@
         ),
         name="green_and_scatter",
     )(energies, counts, strengths, offsets, sigma_in[:, 0], hamiltonian[0], coupling[0])
-    return (1.0 - MIX_RATE) * sigma_in + MIX_RATE * sigma_new.reshape(sigma_in.shape)
+    return (1.0 - MIX_RATE) * sigma_in + sigma_new.reshape(sigma_in.shape)
 
 
 def body(sigma_in, hamiltonian, coupling, energies, counts, strengths, offsets):

time: 115 us -> 104 us (0.904)
  Pallas kernels: 109 us -> 98.9 us
    pallas_call x1, Pallas kernels: 109 us -> 98.9 us  [fused_body(): pl.pallas_call(functools.partial(kernel, ranks, moments, points, order, h...]
    mul x1 -> x0, other arithmetic: 1.96 us -> none  [fused_body(): MIX_RATE * sigma_new.reshape(sigma_in.shape)]
    add x1, other arithmetic: 1.67 us -> 3.18 us  [fused_body(): return (1.0 - MIX_RATE) * sigma_in + sigma_new.reshape(sigma_in.shape)]
where the time goes in v2:
time: 104 us; the launch traced here: 102 us
  Pallas kernels  98.9 us (95%)
  other arithmetic  3.18 us (3%)
    pallas_call x1, Pallas kernels, fused_body(): pl.pallas_call(functools.partial(kernel, ranks, moments, points, order, h...  98.9 us
    add x1, other arithmetic, fused_body(): return (1.0 - MIX_RATE) * sigma_in + sigma_new.reshape(sigma_in.shape)  3.18 us

profile of v2, /device:TPU:1, one launch (start us, length us, event | category | flops | bytes accessed | tf_op | source)
XLA Modules:
  0.0 102.1 jit_solution(13785010881999071386)
XLA Ops:
  0.0 0.0 copy-start
  0.0 98.9 %green_and_scatter.1 = f32[4,64,8,256]{3,2,1,0:T(8,128)} custom-call(f32[64]{0:T(128)} %energy_ref.1, s32[64]{0:T(128)} %count_ref.1, f32[16]{0:T(128)} %strength_ref.1, s32[16]{0:T(128)} %offset_ref.1, f32[4,2,256,256]{3,2,1,0:T(8,128)} %bitcast.6, f32[2,256,256]{2,1,0:T(8,128)} %bitcast.8, f32[256,256]{1,0:T(8,128)} %bitcast.9), custom_call_target="tpu_custom_call" | custom-call | tf_op jit(solution)/shard_map/green_and_scatter/pallas_call | solution.py:308
  98.9 0.0 copy-done
  98.9 3.2 %multiply_add_fusion = f32[4,1,2,256,256]{4,3,2,1,0:T(8,128)} fusion(f32[4,1,2,256,256]{4,3,2,1,0:T(8,128)} %bitcast.7, f32[4,1,2,256,256]{4,3,2,1,0:T(8,128)S(1)} %copy-done), kind=kLoop, calls=%fused_computation | loop fusion | flops 1048576 | bytes 6291456 | tf_op jit(solution)/shard_map/add | solution.py:330
Async XLA Ops:
  0.0 98.9 %copy-start = (f32[4,1,2,256,256]{4,3,2,1,0:T(8,128)S(1)}, f32[4,1,2,256,256]{4,3,2,1,0:T(8,128)}, u32[]{:S(2)}) copy-start(f32[4,1,2,256,256]{4,3,2,1,0:T(8,128)} %param.7) | copy-start | bytes 6291460

commit v3 on v2

--- a/solution.py
+++ b/solution.py
@@ -142,16 +142,22 @@
 
 def kernel(
     ranks, moments, points, order, held,
-    energy_ref, count_ref, strength_ref, offset_ref, sigma_ref, ham_ref, coupling_ref,
+    energy_ref, count_ref, strength_ref, offset_ref, sigma_hbm, ham_ref, coupling_ref,
     out_ref,
     green, gathered, mixed_out, wide, across, across_t,
-    send_first, recv_first, send_second, recv_second,
+    sigma_ref, read_sem, send_first, recv_first, send_second, recv_second,
 ):
     devices = ranks * moments
     total = ranks * points
     my_rank = lax.axis_index("energy")
     my_moment = lax.axis_index("mom")
     me = my_rank * moments + my_moment
+    reads = [
+        pltpu.make_async_copy(sigma_hbm.at[point], sigma_ref.at[point], read_sem.at[point])
+        for point in range(points)
+    ]
+    for read in reads:
+        read.start()
     barrier = pltpu.get_barrier_semaphore()
 
     def greet(index, carried):
@@ -192,6 +198,8 @@
 
     def solve(group, carried):
         chosen = [group * TOGETHER + index for index in range(TOGETHER)]
+        for point in chosen:
+            pltpu.make_async_copy(sigma_hbm.at[point], sigma_ref.at[point], read_sem.at[point]).wait()
         energies = [energy_ref[my_rank * points + point] for point in chosen]
         counts = [count_ref[my_rank * points + point] for point in chosen]
         ratios = [(ham_ref[0] + sigma_ref[point, 0]) * (1.0 / e) for point, e in zip(chosen, energies)]
@@ -308,7 +316,7 @@
     sigma_new = pl.pallas_call(
         functools.partial(kernel, ranks, moments, points, order, held),
         out_shape=jax.ShapeDtypeStruct((points, tiles, SUBLANES, order), jnp.float32),
-        in_specs=[smem] * 4 + [vmem] * 3,
+        in_specs=[smem] * 4 + [pl.BlockSpec(memory_space=pl.ANY)] + [vmem] * 2,
         out_specs=pl.BlockSpec(memory_space=pl.ANY),
         scratch_shapes=[
             pltpu.VMEM((points, tiles, SUBLANES, order), jnp.float32),
@@ -317,6 +325,8 @@
             pltpu.VMEM((span, span), jnp.float32),
             pltpu.VMEM((3 * order, order), jnp.bfloat16),
             pltpu.VMEM((order, 3 * order), jnp.bfloat16),
+            pltpu.VMEM((points, 2, order, order), jnp.float32),
+            pltpu.SemaphoreType.DMA((points,)),
             pltpu.SemaphoreType.DMA,
             pltpu.SemaphoreType.DMA((held,)),
             pltpu.SemaphoreType.DMA,

time: 104 us -> 103 us (level)
  no operation moved by 1% of the time
where the time goes in v3:
time: 103 us; the launch traced here: 102 us
  Pallas kernels  98.5 us (96%)
  other arithmetic  3.18 us (3%)
    pallas_call x1, Pallas kernels, fused_body(): pl.pallas_call(functools.partial(kernel, ranks, moments, points, order, h...  98.5 us
    add x1, other arithmetic, fused_body(): return (1.0 - MIX_RATE) * sigma_in + sigma_new.reshape(sigma_in.shape)  3.18 us

profile of v3, /device:TPU:1, one launch (start us, length us, event | category | flops | bytes accessed | tf_op | source)
XLA Modules:
  0.0 101.7 jit_solution(8195465045457201603)
XLA Ops:
  0.0 0.0 copy-start
  0.0 98.5 %green_and_scatter.1 = f32[4,64,8,256]{3,2,1,0:T(8,128)} custom-call(f32[64]{0:T(128)} %energy_ref.1, s32[64]{0:T(128)} %count_ref.1, f32[16]{0:T(128)} %strength_ref.1, s32[16]{0:T(128)} %offset_ref.1, f32[4,2,256,256]{3,2,1,0:T(8,128)} %bitcast.6, f32[2,256,256]{2,1,0:T(8,128)} %bitcast.8, f32[256,256]{1,0:T(8,128)} %bitcast.9), custom_call_target="tpu_custom_call" | custom-call | tf_op jit(solution)/shard_map/green_and_scatter/pallas_call | solution.py:316
  98.5 0.0 copy-done
  98.5 3.2 %multiply_add_fusion = f32[4,1,2,256,256]{4,3,2,1,0:T(8,128)} fusion(f32[4,1,2,256,256]{4,3,2,1,0:T(8,128)} %bitcast.7, f32[4,1,2,256,256]{4,3,2,1,0:T(8,128)S(1)} %copy-done), kind=kLoop, calls=%fused_computation | loop fusion | flops 1048576 | bytes 6291456 | tf_op jit(solution)/shard_map/add | solution.py:340
Async XLA Ops:
  0.0 98.5 %copy-start = (f32[4,1,2,256,256]{4,3,2,1,0:T(8,128)S(1)}, f32[4,1,2,256,256]{4,3,2,1,0:T(8,128)}, u32[]{:S(2)}) copy-start(f32[4,1,2,256,256]{4,3,2,1,0:T(8,128)} %param.7) | copy-start | bytes 6291460
